TPU v7x, 32 devices: a whole 2x2x4 slice. The times are simulated.
32 devices in a mesh: shape: 8 (over z, x), cls: 4 (over y, core).
Axes of the slice: x: 2, y: 2, z: 4, core: 2. Of those that a mesh axis runs over, the one named last changes fastest.
Arguments:
- shapes: bfloat16 [4096, 1280], P('shape', 'cls'), may hold values from -600 to 600
- classes: bfloat16 [20480, 1280], P('cls'), may hold values from -400 to 400
- counts: int32 [20480], P('cls'), may hold values from 0 to 2, as said below
Outputs:
- assignment: bfloat16 [4096, 20480], P('shape', 'cls')
Inputs may be any that keep to these rules, and one draw needn't show every extreme that they name: The counts sum to 4096; exactly 1024 classes have count 2.
All inputs are finite; a program needn't handle non-finite values.
Results may differ from a plain program's by a relative error of at most 0.001.
Values may be sent and summed in bfloat16 or wider, within the bound.
No kernel may reach another device: no remote copies, remote signals or barrier semaphores. Data moves between devices by JAX's collectives and lax.ppermute only.
A program may use at most 128 MiB of HBM per device.

v0:
```python
import jax
import jax.numpy as jnp
from jax import lax
from jax.sharding import PartitionSpec as P

ITERS = 3
logit_scale = 40.0
epsilon = 1e-06


def row_totals(partial_value):
    return lax.psum(partial_value, "cls")


def shards(shapes, classes, counts):
    class_f = classes.astype(jnp.float32)
    class_scale = lax.rsqrt(jnp.sum(class_f * class_f, axis=1) + epsilon)
    piece = lax.all_gather(shapes, "cls", axis=1, tiled=True)
    term = lax.dot_general(
        piece, classes, (((1,), (1,)), ((), ())), preferred_element_type=jnp.float32
    )
    piece_f = piece.astype(jnp.float32)
    squares = jnp.sum(piece_f * piece_f, axis=1)
    shape_scale = lax.rsqrt(squares + epsilon)
    kernel = jnp.exp(logit_scale * term * shape_scale[:, None] * class_scale[None, :])
    target = counts.astype(jnp.float32)
    row_inv = 1.0 / row_totals(jnp.sum(kernel, axis=1))
    col_scale = jnp.zeros((classes.shape[0],), jnp.float32)
    for step in range(ITERS):
        column_part = jnp.dot(row_inv, kernel, precision=lax.Precision.HIGHEST)
        col_scale = target / lax.psum(column_part, "shape")
        row_inv = 1.0 / row_totals(jnp.dot(kernel, col_scale, precision=lax.Precision.HIGHEST))
    result = row_inv[:, None] * kernel * col_scale[None, :]
    return result.astype(jnp.bfloat16)


def solution(mesh):
    placed = (P("shape", "cls"), P("cls", None), P("cls"))
    return jax.shard_map(
        shards, mesh=mesh, in_specs=placed, out_specs=P("shape", "cls"), check_vma=False
    )
```

profile of v0, /device:TPU:0, one launch (start us, length us, event | category | flops | bytes accessed | tf_op | source)
XLA Modules:
  0.0 246.2 jit_solution(15459654316340277970)
XLA Ops:
  6.5 0.0 all-gather.2.cloned.1.call-start
  6.5 0.7 all-gather.2.cloned.1.call-update
  7.3 7.3 %multiply_reduce_fusion = f32[5120]{0:T(1024)S(1)} fusion(bf16[5120,1280]{1,0:T(8,128)(2,1)} %param.4), kind=kLoop, calls=%fused_computation | loop fusion | flops 19655680 | bytes 13127680 | tf_op jit(solution)/shard_map/reduce_sum | solution.py:17
  14.6 15.2 %all-gather.2.cloned.1.call-done = bf16[512,1280]{0,1:T(8,128)(2,1)} async-done(((bf16[512,320]{0,1:T(8,128)(2,1)}), bf16[512,1280]{0,1:T(8,128)(2,1)}) %all-gather.2.cloned.1.call-update) | async-done | bytes 1310736 | tf_op jit(solution)/shard_map/all_gather | solution.py:18
  29.8 1.7 multiply_reduce_fusion.1
  31.5 16.2 %fusion = (f32[512]{0:T(512)S(1)}, f32[512,5120]{1,0:T(8,128)}) fusion(f32[5120]{0:T(1024)S(1)} %add_rsqrt_fusion, f32[512]{0:T(512)S(1)} %rsqrt_multiply_fusion, bf16[512,1280]{0,1:T(8,128)(2,1)} %all-gather.2.cloned.1.call-done, bf16[5120,1280]{1,0:T(8,128)(2,1)} %param.4), kind=kOutput, calls=%fused_computation.13 | convolution fusion | flops 6718750208 | bytes 24928256 | tf_op jit(solution)/shard_map/dot_general | solution.py:19
  47.7 0.0 copy-start
  47.7 5.9 %psum.49 = f32[512]{0:T(512)S(1)} all-reduce(f32[512]{0:T(512)S(1)} %get-tuple-element.5), channel_id=1, replica_groups=mesh['shape'=8,'cls'=4] {'cls'}, use_global_device_ids=true, to_apply=%region_3.0 | all-reduce | flops 512 | bytes 4096 | tf_op jit(solution)/shard_map/psum | solution.py:12
  53.5 7.6 %fusion.1 = f32[1,5120]{1,0:T(1,128)S(1)} fusion(f32[512,1]{0,1:T(1,128)S(1)} %bitcast.32, f32[512,5120]{1,0:T(8,128)} %get-tuple-element.6), kind=kOutput, calls=%fused_computation.14 | convolution fusion | flops 31457280 | bytes 10508288 | tf_op jit(solution)/shard_map/dot_general | solution.py:30
  61.2 37.2 %psum.50 = f32[5120]{0:T(1024)S(1)} all-reduce(f32[5120]{0:T(1024)S(1)} %bitcast.27), channel_id=1, replica_groups=mesh['shape'=8,'cls'=4] {'shape'}, use_global_device_ids=true, to_apply=%region_4.0 | all-reduce | flops 5120 | bytes 40960 | tf_op jit(solution)/shard_map/psum | solution.py:31
  98.4 0.0 copy-done
  98.4 11.5 %fusion.2 = f32[1,512]{1,0:T(1,128)S(1)} fusion(f32[512,5120]{1,0:T(8,128)} %get-tuple-element.6, f32[5120,1]{0,1:T(1,128)S(1)} %bitcast.30), kind=kOutput, calls=%fused_computation.15 | convolution fusion | flops 31457280 | bytes 10508288 | tf_op jit(solution)/shard_map/dot_general | solution.py:32
  109.9 5.7 %psum.51 = f32[512]{0:T(512)S(1)} all-reduce(f32[512]{0:T(512)S(1)} %bitcast.33), channel_id=1, replica_groups=mesh['shape'=8,'cls'=4] {'cls'}, use_global_device_ids=true, to_apply=%region_5.0 | all-reduce | flops 512 | bytes 4096 | tf_op jit(solution)/shard_map/psum | solution.py:12
  115.6 7.6 %fusion.3 = f32[1,5120]{1,0:T(1,128)S(1)} fusion(f32[512,1]{0,1:T(1,128)S(1)} %bitcast.34, f32[512,5120]{1,0:T(8,128)} %get-tuple-element.6), kind=kOutput, calls=%fused_computation.16 | convolution fusion | flops 31457280 | bytes 10508288 | tf_op jit(solution)/shard_map/dot_general | solution.py:30
  123.2 33.0 %psum.52 = f32[5120]{0:T(1024)S(1)} all-reduce(f32[5120]{0:T(1024)S(1)} %bitcast.28), channel_id=1, replica_groups=mesh['shape'=8,'cls'=4] {'shape'}, use_global_device_ids=true, to_apply=%region_6.0 | all-reduce | flops 5120 | bytes 40960 | tf_op jit(solution)/shard_map/psum | solution.py:31
  156.2 11.5 %fusion.4 = f32[1,512]{1,0:T(1,128)S(1)} fusion(f32[512,5120]{1,0:T(8,128)} %get-tuple-element.6, f32[5120,1]{0,1:T(1,128)S(1)} %bitcast.31), kind=kOutput, calls=%fused_computation.17 | convolution fusion | flops 31457280 | bytes 10508288 | tf_op jit(solution)/shard_map/dot_general | solution.py:32
  167.7 5.9 %psum.53 = f32[512]{0:T(512)S(1)} all-reduce(f32[512]{0:T(512)S(1)} %bitcast.35), channel_id=1, replica_groups=mesh['shape'=8,'cls'=4] {'cls'}, use_global_device_ids=true, to_apply=%region_7.0 | all-reduce | flops 512 | bytes 4096 | tf_op jit(solution)/shard_map/psum | solution.py:12
  173.6 7.6 %fusion.5 = f32[1,5120]{1,0:T(1,128)S(1)} fusion(f32[512,1]{0,1:T(1,128)S(1)} %bitcast.36, f32[512,5120]{1,0:T(8,128)} %get-tuple-element.6), kind=kOutput, calls=%fused_computation.18 | convolution fusion | flops 31457280 | bytes 10508288 | tf_op jit(solution)/shard_map/dot_general | solution.py:30
  181.2 33.0 %psum.54 = f32[5120]{0:T(1024)S(1)} all-reduce(f32[5120]{0:T(1024)S(1)} %bitcast.29), channel_id=1, replica_groups=mesh['shape'=8,'cls'=4] {'shape'}, use_global_device_ids=true, to_apply=%region_8.0 | all-reduce | flops 5120 | bytes 40960 | tf_op jit(solution)/shard_map/psum | solution.py:31
  214.2 11.5 %fusion.6 = f32[1,512]{1,0:T(1,128)S(1)} fusion(f32[512,5120]{1,0:T(8,128)} %get-tuple-element.6, f32[5120,1]{0,1:T(1,128)S(1)} %bitcast.26), kind=kOutput, calls=%fused_computation.19 | convolution fusion | flops 31457280 | bytes 10508288 | tf_op jit(solution)/shard_map/dot_general | solution.py:32
  225.7 5.7 %psum.55 = f32[512]{0:T(512)S(1)} all-reduce(f32[512]{0:T(512)S(1)} %bitcast.37), channel_id=1, replica_groups=mesh['shape'=8,'cls'=4] {'cls'}, use_global_device_ids=true, to_apply=%region_9.0 | all-reduce | flops 512 | bytes 4096 | tf_op jit(solution)/shard_map/psum | solution.py:12
  231.4 8.0 %multiply_convert_fusion = bf16[512,5120]{1,0:T(8,128)(2,1)} fusion(f32[512,5120]{1,0:T(8,128)} %get-tuple-element.6, f32[5120]{0:T(1024)S(1)} %convert_divide_fusion, f32[512]{0:T(512)S(1)} %broadcast_divide_fusion), kind=kLoop, calls=%fused_computation.1 | loop fusion | flops 7864320 | bytes 15751168 | tf_op jit(solution)/shard_map/convert_element_type | solution.py:34
  (9 shorter events, 0.1 us)
Async XLA Ops:
  6.5 23.3 %all-gather.2.cloned.1.call-start = ((), (), s32[]{:S(2)}) async-start(), calls=%async_computation | async-start | bytes 1638400 | tf_op jit(solution)/shard_map/all_gather | solution.py:18
  47.7 50.7 %copy-start = (s32[5120]{0:T(1024)S(1)}, s32[5120]{0:T(1024)}, u32[]{:S(2)}) copy-start(s32[5120]{0:T(1024)} %param.5) | copy-start | bytes 61444
Sparse Core Ops, SparseCore 0:
  8.9 20.8 all-gather.1
where the time goes:
time: 247 us; the launch traced here: 246 us
  blocking collectives  126 us (51%)
  matrix products  73.5 us (30%)
  other arithmetic  17.1 us (7%)
  waiting for transfers between devices  15.9 us (6%)
  between operations  13.4 us (5%)
    psum x3, blocking collectives, shards(): col_scale = target / lax.psum(column_part, 'shape')  103 us
    dot_general x3, matrix products, shards(): jnp.dot(kernel, col_scale, precision=lax.Precision.HIGHEST)  34.4 us
    psum x4, blocking collectives, row_totals(): return lax.psum(partial_value, 'cls')  23 us
    dot_general x3, matrix products, shards(): column_part = jnp.dot(row_inv, kernel, precision=lax.Precision.HIGHEST)  22.9 us
    dot_general x1, matrix products, shards(): lax.dot_general(piece, classes, (((1,), (1,)), ((), ())), preferred_eleme...  16.2 us
    all_gather x1, waiting for transfers between devices, shards(): piece = lax.all_gather(shapes, 'cls', axis=1, tiled=True)  15.2 us
    convert_element_type x1, other arithmetic, shards(): return result.astype(jnp.bfloat16)  8 us
    reduce_sum x1, other arithmetic, shards(): class_scale = lax.rsqrt(jnp.sum(class_f * class_f, axis=1) + epsilon)  7.35 us
  transfers between devices with their start and end apart: 1, of which 1 were waited for; matrix products, arithmetic and copies ran while one was open for 3% of the time, Pallas kernels for 0%

commit v1 on v0

--- a/solution.py
+++ b/solution.py
@@ -15,7 +15,8 @@
 def shards(shapes, classes, counts):
     class_f = classes.astype(jnp.float32)
     class_scale = lax.rsqrt(jnp.sum(class_f * class_f, axis=1) + epsilon)
-    piece = lax.all_gather(shapes, "cls", axis=1, tiled=True)
+    repeated = jnp.stack([shapes] * lax.axis_size("cls"))
+    piece = jnp.concatenate(lax.all_to_all(repeated, "cls", 0, 0), axis=1)
     term = lax.dot_general(
         piece, classes, (((1,), (1,)), ((), ())), preferred_element_type=jnp.float32
     )

time: 247 us -> 231 us (0.935)
  between operations: 13.4 us -> 0.02 us
  waiting for transfers between devices: 15.9 us -> 9.88 us
  starting transfers between devices: 0.01 us -> 4.26 us
    all_gather x1 -> x0, waiting for transfers between devices: 15.2 us -> none  [shards(): piece = lax.all_gather(shapes, 'cls', axis=1, tiled=True)]
    all_to_all x0 -> x1, waiting for transfers between devices: none -> 9.88 us  [shards(): piece = jnp.concatenate(lax.all_to_all(repeated, 'cls', 0, 0), axis=1)]
    all_to_all x0 -> x1, starting transfers between devices: none -> 4.26 us  [shards(): piece = jnp.concatenate(lax.all_to_all(repeated, 'cls', 0, 0), axis=1)]
where the time goes in v1:
time: 231 us
  blocking collectives  127 us (55%)
  matrix products  71.3 us (31%)
  other arithmetic  15.8 us (7%)
  waiting for transfers between devices  9.88 us (4%)
  starting transfers between devices  4.26 us (2%)
    psum x3, blocking collectives, shards(): col_scale = target / lax.psum(column_part, 'shape')  104 us
    dot_general x3, matrix products, shards(): jnp.dot(kernel, col_scale, precision=lax.Precision.HIGHEST)  34.4 us
    psum x4, blocking collectives, row_totals(): return lax.psum(partial_value, 'cls')  23.1 us
    dot_general x3, matrix products, shards(): column_part = jnp.dot(row_inv, kernel, precision=lax.Precision.HIGHEST)  22.9 us
    dot_general x1, matrix products, shards(): lax.dot_general(piece, classes, (((1,), (1,)), ((), ())), preferred_eleme...  14 us
    all_to_all x1, waiting for transfers between devices, shards(): piece = jnp.concatenate(lax.all_to_all(repeated, 'cls', 0, 0), axis=1)  9.88 us
    convert_element_type x1, other arithmetic, shards(): return result.astype(jnp.bfloat16)  8 us
    reduce_sum x1, other arithmetic, shards(): class_scale = lax.rsqrt(jnp.sum(class_f * class_f, axis=1) + epsilon)  7.35 us
  transfers between devices with their start and end apart: 1, of which 1 were waited for; matrix products, arithmetic and copies ran while one was open for 3% of the time, Pallas kernels for 0%

profile of v1, /device:TPU:0, one launch (start us, length us, event | category | flops | bytes accessed | tf_op | source)
XLA Modules:
  0.0 230.5 jit_solution(6281954552882883272)
XLA Ops:
  0.0 2.1 stack.2
  2.1 4.3 %all-to-all-start = ((bf16[4,512,320]{1,2,0:T(8,128)(2,1)}), bf16[4,512,320]{1,2,0:T(8,128)(2,1)S(1)}, u32[]{:S(2)}, u32[]{:S(2)}) async-start(bf16[4,512,320]{1,2,0:T(8,128)(2,1)} %stack.2), calls=%async_computation | async-start | bytes 2621440 | tf_op jit(solution)/shard_map/all_to_all | solution.py:19
  6.4 7.3 %multiply_reduce_fusion = f32[5120]{0:T(1024)S(1)} fusion(bf16[5120,1280]{1,0:T(8,128)(2,1)} %param.4), kind=kLoop, calls=%fused_computation | loop fusion | flops 19655680 | bytes 13127680 | tf_op jit(solution)/shard_map/reduce_sum | solution.py:17
  13.8 9.9 %all-to-all-done = bf16[4,512,320]{1,2,0:T(8,128)(2,1)S(1)} async-done(((bf16[4,512,320]{1,2,0:T(8,128)(2,1)}), bf16[4,512,320]{1,2,0:T(8,128)(2,1)S(1)}, u32[]{:S(2)}, u32[]{:S(2)}) %all-to-all-start) | async-done | bytes 1310752 | tf_op jit(solution)/shard_map/all_to_all | solution.py:19
  23.6 0.3 multiply_reduce_fusion.1
  24.0 14.0 %fusion = (f32[512]{0:T(512)S(1)}, f32[512,5120]{1,0:T(8,128)}) fusion(f32[5120]{0:T(1024)S(1)} %add_rsqrt_fusion, f32[512]{0:T(512)S(1)} %rsqrt_multiply_fusion, bf16[512,1280]{0,1:T(8,128)(2,1)S(1)} %bitcast.30, bf16[5120,1280]{1,0:T(8,128)(2,1)} %param.4), kind=kOutput, calls=%fused_computation.13 | convolution fusion | flops 6718750208 | bytes 24928256 | tf_op jit(solution)/shard_map/dot_general | solution.py:20
  38.0 0.0 copy-start
  38.0 5.9 %psum.49 = f32[512]{0:T(512)S(1)} all-reduce(f32[512]{0:T(512)S(1)} %get-tuple-element.5), channel_id=1, replica_groups=mesh['shape'=8,'cls'=4] {'cls'}, use_global_device_ids=true, to_apply=%region_3.0 | all-reduce | flops 512 | bytes 4096 | tf_op jit(solution)/shard_map/psum | solution.py:12
  43.9 7.6 %fusion.1 = f32[1,5120]{1,0:T(1,128)S(1)} fusion(f32[512,1]{0,1:T(1,128)S(1)} %bitcast.37, f32[512,5120]{1,0:T(8,128)} %get-tuple-element.6), kind=kOutput, calls=%fused_computation.14 | convolution fusion | flops 31457280 | bytes 10508288 | tf_op jit(solution)/shard_map/dot_general | solution.py:31
  51.5 38.1 %psum.50 = f32[5120]{0:T(1024)S(1)} all-reduce(f32[5120]{0:T(1024)S(1)} %bitcast.32), channel_id=1, replica_groups=mesh['shape'=8,'cls'=4] {'shape'}, use_global_device_ids=true, to_apply=%region_4.0 | all-reduce | flops 5120 | bytes 40960 | tf_op jit(solution)/shard_map/psum | solution.py:32
  89.6 0.0 copy-done
  89.6 11.5 %fusion.2 = f32[1,512]{1,0:T(1,128)S(1)} fusion(f32[512,5120]{1,0:T(8,128)} %get-tuple-element.6, f32[5120,1]{0,1:T(1,128)S(1)} %bitcast.35), kind=kOutput, calls=%fused_computation.15 | convolution fusion | flops 31457280 | bytes 10508288 | tf_op jit(solution)/shard_map/dot_general | solution.py:33
  101.1 5.7 %psum.51 = f32[512]{0:T(512)S(1)} all-reduce(f32[512]{0:T(512)S(1)} %bitcast.38), channel_id=1, replica_groups=mesh['shape'=8,'cls'=4] {'cls'}, use_global_device_ids=true, to_apply=%region_5.0 | all-reduce | flops 512 | bytes 4096 | tf_op jit(solution)/shard_map/psum | solution.py:12
  106.7 7.6 %fusion.3 = f32[1,5120]{1,0:T(1,128)S(1)} fusion(f32[512,1]{0,1:T(1,128)S(1)} %bitcast.39, f32[512,5120]{1,0:T(8,128)} %get-tuple-element.6), kind=kOutput, calls=%fused_computation.16 | convolution fusion | flops 31457280 | bytes 10508288 | tf_op jit(solution)/shard_map/dot_general | solution.py:31
  114.4 33.0 %psum.52 = f32[5120]{0:T(1024)S(1)} all-reduce(f32[5120]{0:T(1024)S(1)} %bitcast.33), channel_id=1, replica_groups=mesh['shape'=8,'cls'=4] {'shape'}, use_global_device_ids=true, to_apply=%region_6.0 | all-reduce | flops 5120 | bytes 40960 | tf_op jit(solution)/shard_map/psum | solution.py:32
  147.4 11.5 %fusion.4 = f32[1,512]{1,0:T(1,128)S(1)} fusion(f32[512,5120]{1,0:T(8,128)} %get-tuple-element.6, f32[5120,1]{0,1:T(1,128)S(1)} %bitcast.36), kind=kOutput, calls=%fused_computation.17 | convolution fusion | flops 31457280 | bytes 10508288 | tf_op jit(solution)/shard_map/dot_general | solution.py:33
  158.9 5.9 %psum.53 = f32[512]{0:T(512)S(1)} all-reduce(f32[512]{0:T(512)S(1)} %bitcast.40), channel_id=1, replica_groups=mesh['shape'=8,'cls'=4] {'cls'}, use_global_device_ids=true, to_apply=%region_7.0 | all-reduce | flops 512 | bytes 4096 | tf_op jit(solution)/shard_map/psum | solution.py:12
  164.7 7.6 %fusion.5 = f32[1,5120]{1,0:T(1,128)S(1)} fusion(f32[512,1]{0,1:T(1,128)S(1)} %bitcast.41, f32[512,5120]{1,0:T(8,128)} %get-tuple-element.6), kind=kOutput, calls=%fused_computation.18 | convolution fusion | flops 31457280 | bytes 10508288 | tf_op jit(solution)/shard_map/dot_general | solution.py:31
  172.4 33.0 %psum.54 = f32[5120]{0:T(1024)S(1)} all-reduce(f32[5120]{0:T(1024)S(1)} %bitcast.34), channel_id=1, replica_groups=mesh['shape'=8,'cls'=4] {'shape'}, use_global_device_ids=true, to_apply=%region_8.0 | all-reduce | flops 5120 | bytes 40960 | tf_op jit(solution)/shard_map/psum | solution.py:32
  205.4 11.5 %fusion.6 = f32[1,512]{1,0:T(1,128)S(1)} fusion(f32[512,5120]{1,0:T(8,128)} %get-tuple-element.6, f32[5120,1]{0,1:T(1,128)S(1)} %bitcast.31), kind=kOutput, calls=%fused_computation.19 | convolution fusion | flops 31457280 | bytes 10508288 | tf_op jit(solution)/shard_map/dot_general | solution.py:33
  216.9 5.7 %psum.55 = f32[512]{0:T(512)S(1)} all-reduce(f32[512]{0:T(512)S(1)} %bitcast.42), channel_id=1, replica_groups=mesh['shape'=8,'cls'=4] {'cls'}, use_global_device_ids=true, to_apply=%region_9.0 | all-reduce | flops 512 | bytes 4096 | tf_op jit(solution)/shard_map/psum | solution.py:12
  222.5 8.0 %multiply_convert_fusion = bf16[512,5120]{1,0:T(8,128)(2,1)} fusion(f32[512,5120]{1,0:T(8,128)} %get-tuple-element.6, f32[5120]{0:T(1024)S(1)} %convert_divide_fusion, f32[512]{0:T(512)S(1)} %broadcast_divide_fusion), kind=kLoop, calls=%fused_computation.1 | loop fusion | flops 7864320 | bytes 15751168 | tf_op jit(solution)/shard_map/convert_element_type | solution.py:35
  (9 shorter events, 0.1 us)
Async XLA Ops:
  2.1 21.5 %all-to-all-start = ((bf16[4,512,320]{1,2,0:T(8,128)(2,1)}), bf16[4,512,320]{1,2,0:T(8,128)(2,1)S(1)}, u32[]{:S(2)}, u32[]{:S(2)}) async-start(bf16[4,512,320]{1,2,0:T(8,128)(2,1)} %stack.2), calls=%async_computation | async-start | bytes 2621440 | tf_op jit(solution)/shard_map/all_to_all | solution.py:19
  38.0 51.6 %copy-start = (s32[5120]{0:T(1024)S(1)}, s32[5120]{0:T(1024)}, u32[]{:S(2)}) copy-start(s32[5120]{0:T(1024)} %param.5) | copy-start | bytes 61444
